TPU v7x, 32 devices: a whole 2x2x4 slice. The times are simulated.
32 devices in a mesh: rows: 8 (over z, core), pairs: 4 (over y, x).
Axes of the slice: x: 2, y: 2, z: 4, core: 2. Of those that a mesh axis runs over, the one named last changes fastest.
Arguments:
- observed: float32 [12288, 2048], P('rows', 'pairs'), as said below
- estimate: float32 [12288, 2048], P('rows', 'pairs'), may hold values from -0.054126587 to 0.054126587
- mask: int32 [12288, 2048], P('rows', 'pairs'), may hold values from 0 to 1
- threshold: float32 [2048], P('pairs'), may hold values from 0.02 to 0.12
Outputs:
- regrouped: float32 [2048, 12288], P(('rows', 'pairs'))
Inputs may be any that keep to these rules, and one draw needn't show every extreme that they name: observed has entries of order 12288^-1/2.
All inputs are finite; a program needn't handle non-finite values.
Results may differ from a plain program's by a relative error of at most 0.0003.
Values sent between devices are 32-bit elements; how exact they have to be, the bound alone decides.
A program may use at most 128 MiB of HBM per device.

v0:
```python
import jax
import jax.numpy as jnp
from jax import lax
from jax.sharding import PartitionSpec as P

ROUNDS = 4
NS_STEPS = 3
HI = lax.Precision.HIGHEST


def from_behind(block, axis, distance):
    devices = range(lax.axis_size(axis))
    route = [((i - distance) % len(devices), i) for i in devices]
    return lax.ppermute(block, axis, route)


def whitening_of(gram):
    width = gram.shape[-1]
    eye = jnp.eye(width, dtype=jnp.float32)
    dsum = jnp.diagonal(gram, axis1=-2, axis2=-1) + 1e-06
    inv_root = 1.0 / jnp.sqrt(dsum)
    normed = gram * inv_root[..., :, None] * inv_root[..., None, :]
    fro = jnp.sqrt(jnp.sum(normed * normed, axis=(-2, -1)))
    ymat = normed / fro[..., None, None]
    zmat = jnp.broadcast_to(eye, normed.shape)
    for step in range(NS_STEPS):
        tmat = 1.5 * eye - 0.5 * jnp.einsum("pij,pjk->pik", zmat, ymat, precision=HI)
        ymat = jnp.einsum("pij,pjk->pik", ymat, tmat, precision=HI)
        zmat = jnp.einsum("pij,pjk->pik", tmat, zmat, precision=HI)
    return (
        inv_root[..., :, None]
        * zmat
        * jnp.sqrt(dsum)[..., None, :]
        / jnp.sqrt(fro)[..., None, None]
    )


def on_device(observed, estimate, mask, threshold):
    filled = jnp.where(mask == 1, observed, estimate)
    rows_here, width = filled.shape
    block = width // 4
    for round_index in range(ROUNDS):
        pairs = filled.reshape(rows_here, 2, 2 * block)
        partial_gram = jnp.einsum("rpi,rpj->pij", pairs, pairs, precision=HI)
        gram = lax.psum(partial_gram, "rows")
        whitening = whitening_of(gram)
        pairs = jnp.einsum("rpi,pij->rpj", pairs, whitening, precision=HI)
        quads = pairs.reshape(rows_here, 4, block)
        if round_index + 1 < ROUNDS:
            moved = from_behind(quads[:, 3], "pairs", 1)
            quads = jnp.stack([quads[:, 0], moved, quads[:, 2], quads[:, 1]], axis=1)
        filled = quads.reshape(rows_here, width)
    squares = lax.psum(jnp.sum(filled * filled, axis=0), "rows")
    col_norm = jnp.sqrt(squares + 1e-06)
    factor = jnp.maximum(col_norm - threshold, 0.0) / col_norm
    shrunk_t = (filled * factor[None, :]).T
    count_rows = lax.axis_size("rows")
    count_pairs = lax.axis_size("pairs")
    each_dest = width // (count_rows * count_pairs)
    packed = shrunk_t.reshape(count_rows * count_pairs, each_dest, rows_here)
    landed = lax.all_to_all(packed, ("rows", "pairs"), split_axis=0, concat_axis=1, tiled=True)
    landed = landed.reshape(count_rows, count_pairs, each_dest, rows_here).transpose(2, 1, 0, 3)
    return landed.reshape(each_dest * count_pairs, count_rows * rows_here)


def solution(mesh):
    placed = (P("rows", "pairs"), P("rows", "pairs"), P("rows", "pairs"), P("pairs"))
    return jax.shard_map(
        on_device, mesh=mesh, in_specs=placed, out_specs=P(("rows", "pairs"), None), check_vma=False
    )
```

profile of v0, /device:TPU:0, one launch (start us, length us, event | category | flops | bytes accessed | tf_op | source)
XLA Modules:
  0.0 571.2 jit_solution(13144928827066859881)
XLA Ops:
  6.5 4.9 compare_select_fusion
  11.4 6.2 %fusion.2 = f32[2,256,256]{2,1,0:T(8,128)} fusion(f32[192,2,8,256]{3,2,1,0:T(8,128)S(1)} %bitcast.133), kind=kOutput, calls=%fused_computation.6 | convolution fusion | flops 2415919104 | bytes 3670016 | tf_op jit(solution)/shard_map/rpi,rpj->pij/dot_general | solution.py:44
  18.5 58.6 %all-reduce.5.cloned.1.call-done = f32[2,256,256]{2,1,0:T(8,128)} async-done(((f32[2,256,256]{2,1,0:T(8,128)}), f32[2,256,256]{2,1,0:T(8,128)}) %all-reduce.5.cloned.1.call-update) | async-done | bytes 524304 | tf_op jit(solution)/shard_map/psum | solution.py:45
  77.0 17.5 %copy.62 = f32[2,256,256]{0,2,1:T(8,128)} copy(f32[2,256,256]{2,1,0:T(8,128)} %all-reduce.5.cloned.1.call-done) | data formatting | bytes 1048576 | tf_op jit(solution)/shard_map/psum | solution.py:45
  94.5 3.0 gather_fusion
  101.5 1.9 fusion.26
  112.0 5.3 fusion
  119.1 16.9 %collective-permute-done = f32[1536,128]{0,1:T(8,128)S(1)} collective-permute-done((f32[1536,128]{0,1:T(8,128)S(1)}, f32[1536,128]{0,1:T(8,128)S(1)}, u32[]{:S(2)}, u32[]{:S(2)}) %collective-permute-start) | collective-permute-done | bytes 786464 | tf_op jit(solution)/shard_map/ppermute | solution.py:14
  136.4 3.9 fusion.62
  140.8 55.3 %all-reduce.7.cloned.1.call-done = f32[2,256,256]{2,1,0:T(8,128)} async-done(((f32[2,256,256]{2,1,0:T(8,128)}), f32[2,256,256]{2,1,0:T(8,128)}) %all-reduce.7.cloned.1.call-update) | async-done | bytes 524304 | tf_op jit(solution)/shard_map/psum | solution.py:45
  196.0 17.3 %copy.69 = f32[2,256,256]{0,2,1:T(8,128)} copy(f32[2,256,256]{2,1,0:T(8,128)} %all-reduce.7.cloned.1.call-done) | data formatting | bytes 1048576 | tf_op jit(solution)/shard_map/psum | solution.py:45
  213.3 3.0 gather_fusion.1
  220.2 1.9 fusion.21
  230.7 3.1 fusion.65
  235.8 16.9 %collective-permute-done.1 = f32[1536,128]{0,1:T(8,128)S(1)} collective-permute-done((f32[1536,128]{0,1:T(8,128)S(1)}, f32[1536,128]{0,1:T(8,128)S(1)}, u32[]{:S(2)}, u32[]{:S(2)}) %collective-permute-start.1) | collective-permute-done | bytes 786464 | tf_op jit(solution)/shard_map/ppermute | solution.py:14
  253.0 3.9 fusion.66
  257.0 55.7 %all-reduce.9.cloned.1.call-done = f32[2,256,256]{2,1,0:T(8,128)} async-done(((f32[2,256,256]{2,1,0:T(8,128)}), f32[2,256,256]{2,1,0:T(8,128)}) %all-reduce.9.cloned.1.call-update) | async-done | bytes 524304 | tf_op jit(solution)/shard_map/psum | solution.py:45
  312.6 17.3 %copy.76 = f32[2,256,256]{0,2,1:T(8,128)} copy(f32[2,256,256]{2,1,0:T(8,128)} %all-reduce.9.cloned.1.call-done) | data formatting | bytes 1048576 | tf_op jit(solution)/shard_map/psum | solution.py:45
  329.9 3.0 gather_fusion.2
  336.9 1.9 fusion.16
  347.4 3.1 fusion.69
  352.5 16.9 %collective-permute-done.2 = f32[1536,128]{0,1:T(8,128)S(1)} collective-permute-done((f32[1536,128]{0,1:T(8,128)S(1)}, f32[1536,128]{0,1:T(8,128)S(1)}, u32[]{:S(2)}, u32[]{:S(2)}) %collective-permute-start.2) | collective-permute-done | bytes 786464 | tf_op jit(solution)/shard_map/ppermute | solution.py:14
  369.7 3.9 fusion.70
  373.6 55.7 %all-reduce.11.cloned.1.call-done = f32[2,256,256]{2,1,0:T(8,128)} async-done(((f32[2,256,256]{2,1,0:T(8,128)}), f32[2,256,256]{2,1,0:T(8,128)}) %all-reduce.11.cloned.1.call-update) | async-done | bytes 524304 | tf_op jit(solution)/shard_map/psum | solution.py:45
  429.3 17.3 %copy.83 = f32[2,256,256]{0,2,1:T(8,128)} copy(f32[2,256,256]{2,1,0:T(8,128)} %all-reduce.11.cloned.1.call-done) | data formatting | bytes 1048576 | tf_op jit(solution)/shard_map/psum | solution.py:45
  446.6 3.0 gather_fusion.3
  453.5 1.9 fusion.11
  464.1 4.7 fusion.4
  468.8 13.7 %psum.39 = f32[512]{0:T(512)S(1)} all-reduce(f32[512]{0:T(512)S(1)} %bitcast.145), channel_id=1, replica_groups=mesh['rows'=8,'pairs'=4] {'rows'}, use_global_device_ids=true, to_apply=%region_9.10 | all-reduce | flops 512 | bytes 4096 | tf_op jit(solution)/shard_map/psum | solution.py:53
  482.5 2.2 bitcast_multiply_fusion
  484.7 74.3 %all_to_all.4 = f32[32,16,1536]{2,1,0:T(8,128)S(1)} all-to-all(f32[32,16,1536]{2,1,0:T(8,128)S(1)} %bitcast.135), channel_id=1, replica_groups=mesh['rows'=8,'pairs'=4] {'rows','pairs'}, dimensions={0} | all-to-all | bytes 6291456 | tf_op jit(solution)/shard_map/all_to_all | solution.py:61
  560.8 3.4 copy.102
  (89 shorter events, 60.0 us)
Async XLA Ops:
  6.5 70.5 %all-reduce.5.cloned.1.call-start = ((), (), s32[]{:S(2)}) async-start(), calls=%async_computation.1 | async-start | bytes 1048576 | tf_op jit(solution)/shard_map/psum | solution.py:45
  17.7 178.4 %all-reduce.7.cloned.1.call-start = ((), (), s32[]{:S(2)}) async-start(), calls=%async_computation.2 | async-start | bytes 1048576 | tf_op jit(solution)/shard_map/psum | solution.py:45
  100.1 3.3 copy-start
  100.1 3.9 copy-start.4
  117.6 18.5 %collective-permute-start = (f32[1536,128]{0,1:T(8,128)S(1)}, f32[1536,128]{0,1:T(8,128)S(1)}, u32[]{:S(2)}, u32[]{:S(2)}) collective-permute-start(f32[1536,128]{0,1:T(8,128)S(1)} %get-tuple-element.16), channel_id=1, source_target_pairs={{3,0},{0,1},{1,2},{2,3},{7,4},{4,5},{5,6},{6,7},{11,8},{8,9},{9,10... | collective-permute-start | bytes 2359304 | tf_op jit(solution)/shard_map/ppermute | solution.py:14
  140.2 172.4 %all-reduce.9.cloned.1.call-start = ((), (), s32[]{:S(2)}) async-start(), calls=%async_computation.3 | async-start | bytes 1048576 | tf_op jit(solution)/shard_map/psum | solution.py:45
  218.8 3.3 copy-start.1
  218.8 3.9 copy-start.5
  234.1 18.6 %collective-permute-start.1 = (f32[1536,128]{0,1:T(8,128)S(1)}, f32[1536,128]{0,1:T(8,128)S(1)}, u32[]{:S(2)}, u32[]{:S(2)}) collective-permute-start(f32[1536,128]{0,1:T(8,128)S(1)} %get-tuple-element.12), channel_id=1, source_target_pairs={{3,0},{0,1},{1,2},{2,3},{7,4},{4,5},{5,6},{6,7},{11,8},{8,9},{9,10... | collective-permute-start | bytes 2359304 | tf_op jit(solution)/shard_map/ppermute | solution.py:14
  256.9 172.4 %all-reduce.11.cloned.1.call-start = ((), (), s32[]{:S(2)}) async-start(), calls=%async_computation.4 | async-start | bytes 1048576 | tf_op jit(solution)/shard_map/psum | solution.py:45
  335.5 3.3 copy-start.2
  335.5 3.9 copy-start.6
  350.7 18.7 %collective-permute-start.2 = (f32[1536,128]{0,1:T(8,128)S(1)}, f32[1536,128]{0,1:T(8,128)S(1)}, u32[]{:S(2)}, u32[]{:S(2)}) collective-permute-start(f32[1536,128]{0,1:T(8,128)S(1)} %get-tuple-element.8), channel_id=1, source_target_pairs={{3,0},{0,1},{1,2},{2,3},{7,4},{4,5},{5,6},{6,7},{11,8},{8,9},{9,10... | collective-permute-start | bytes 2359304 | tf_op jit(solution)/shard_map/ppermute | solution.py:14
  452.1 3.3 copy-start.3
  452.1 3.9 copy-start.7
  464.0 18.4 %copy-start.8 = (f32[512]{0:T(512)S(1)}, f32[512]{0:T(512)}, u32[]{:S(2)}) copy-start(f32[512]{0:T(512)} %param.7) | copy-start | bytes 6148
Sparse Core Ops, SparseCore 0:
  17.8 59.2 all-reduce.4
  140.4 55.6 all-reduce.6
  257.0 55.5 all-reduce.8
  373.7 55.5 all-reduce.10
where the time goes:
time: 579 us; the launch traced here: 571 us
  waiting for transfers between devices  276 us (48%)
  local copies, waits for them, and re-layouts  91.6 us (16%)
  blocking collectives  88 us (15%)
  matrix products  75.5 us (13%)
  other arithmetic  20.6 us (4%)
  between operations  14 us (2%)
    psum x4, waiting for transfers between devices, on_device(): gram = lax.psum(partial_gram, 'rows')  225 us
    all_to_all x1, blocking collectives, on_device(): lax.all_to_all(packed, ('rows', 'pairs'), split_axis=0, concat_axis=1, ti...  74.3 us
    psum x4, local copies, waits for them, and re-layouts, on_device(): gram = lax.psum(partial_gram, 'rows')  69.3 us
    ppermute x3, waiting for transfers between devices, from_behind(): return lax.ppermute(block, axis, route)  50.8 us
    dot_general x4, matrix products, on_device(): partial_gram = jnp.einsum('rpi,rpj->pij', pairs, pairs, precision=HI)  17.7 us
    dot_general x12, matrix products, whitening_of(): jnp.einsum('pij,pjk->pik', zmat, ymat, precision=HI)  17.6 us
    dot_general x4, matrix products, on_device(): pairs = jnp.einsum('rpi,pij->rpj', pairs, whitening, precision=HI)  16.3 us
    dot_general x12, matrix products, whitening_of(): zmat = jnp.einsum('pij,pjk->pik', tmat, zmat, precision=HI)  15.2 us
  transfers between devices with their start and end apart: 7, of which 7 were waited for; matrix products, arithmetic and copies ran while one was open for 0% of the time, Pallas kernels for 0%

commit v1 on v0

--- a/solution.py
+++ b/solution.py
@@ -58,7 +58,10 @@
     count_pairs = lax.axis_size("pairs")
     each_dest = width // (count_rows * count_pairs)
     packed = shrunk_t.reshape(count_rows * count_pairs, each_dest, rows_here)
-    landed = lax.all_to_all(packed, ("rows", "pairs"), split_axis=0, concat_axis=1, tiled=True)
+    size = lax.axis_size(("rows", "pairs"))
+    pieces = jnp.stack(jnp.split(packed, size, axis=0), axis=0)
+    pieces = lax.all_to_all(pieces, ("rows", "pairs"), split_axis=0, concat_axis=0)
+    landed = jnp.concatenate(pieces, axis=1)
     landed = landed.reshape(count_rows, count_pairs, each_dest, rows_here).transpose(2, 1, 0, 3)
     return landed.reshape(each_dest * count_pairs, count_rows * rows_here)
 

time: 579 us -> 579 us (level)
  no operation moved by 1% of the time
where the time goes in v1:
time: 579 us; the launch traced here: 571 us
  waiting for transfers between devices  276 us (48%)
  local copies, waits for them, and re-layouts  91.6 us (16%)
  blocking collectives  88 us (15%)
  matrix products  75.7 us (13%)
  other arithmetic  20.3 us (4%)
  between operations  14.2 us (2%)
    psum x4, waiting for transfers between devices, on_device(): gram = lax.psum(partial_gram, 'rows')  225 us
    all_to_all x1, blocking collectives, on_device(): lax.all_to_all(pieces, ('rows', 'pairs'), split_axis=0, concat_axis=0)  74.3 us
    psum x4, local copies, waits for them, and re-layouts, on_device(): gram = lax.psum(partial_gram, 'rows')  69.3 us
    ppermute x3, waiting for transfers between devices, from_behind(): return lax.ppermute(block, axis, route)  50.8 us
    dot_general x4, matrix products, on_device(): partial_gram = jnp.einsum('rpi,rpj->pij', pairs, pairs, precision=HI)  17.8 us
    dot_general x12, matrix products, whitening_of(): jnp.einsum('pij,pjk->pik', zmat, ymat, precision=HI)  17.7 us
    dot_general x4, matrix products, on_device(): pairs = jnp.einsum('rpi,pij->rpj', pairs, whitening, precision=HI)  16.3 us
    dot_general x12, matrix products, whitening_of(): zmat = jnp.einsum('pij,pjk->pik', tmat, zmat, precision=HI)  15.3 us
  transfers between devices with their start and end apart: 7, of which 7 were waited for; matrix products, arithmetic and copies ran while one was open for 0% of the time, Pallas kernels for 0%

profile of v1, /device:TPU:0, one launch (start us, length us, event | category | flops | bytes accessed | tf_op | source)
XLA Modules:
  0.0 571.5 jit_solution(684438693749981556)
XLA Ops:
  6.5 4.9 compare_select_fusion
  11.4 6.2 %fusion.2 = f32[2,256,256]{2,1,0:T(8,128)} fusion(f32[192,2,8,256]{3,2,1,0:T(8,128)S(1)} %bitcast.258), kind=kOutput, calls=%fused_computation.6 | convolution fusion | flops 2415919104 | bytes 3670016 | tf_op jit(solution)/shard_map/rpi,rpj->pij/dot_general | solution.py:44
  18.5 58.6 %all-reduce.5.cloned.1.call-done = f32[2,256,256]{2,1,0:T(8,128)} async-done(((f32[2,256,256]{2,1,0:T(8,128)}), f32[2,256,256]{2,1,0:T(8,128)}) %all-reduce.5.cloned.1.call-update) | async-done | bytes 524304 | tf_op jit(solution)/shard_map/psum | solution.py:45
  77.1 17.5 %copy.34 = f32[2,256,256]{0,2,1:T(8,128)} copy(f32[2,256,256]{2,1,0:T(8,128)} %all-reduce.5.cloned.1.call-done) | data formatting | bytes 1048576 | tf_op jit(solution)/shard_map/psum | solution.py:45
  94.5 3.0 gather_fusion
  101.5 1.9 fusion.26
  112.0 5.4 fusion
  119.1 16.9 %collective-permute-done = f32[1536,128]{0,1:T(8,128)S(1)} collective-permute-done((f32[1536,128]{0,1:T(8,128)S(1)}, f32[1536,128]{0,1:T(8,128)S(1)}, u32[]{:S(2)}, u32[]{:S(2)}) %collective-permute-start) | collective-permute-done | bytes 786464 | tf_op jit(solution)/shard_map/ppermute | solution.py:14
  136.3 3.9 fusion.94
  140.7 55.3 %all-reduce.7.cloned.1.call-done = f32[2,256,256]{2,1,0:T(8,128)} async-done(((f32[2,256,256]{2,1,0:T(8,128)}), f32[2,256,256]{2,1,0:T(8,128)}) %all-reduce.7.cloned.1.call-update) | async-done | bytes 524304 | tf_op jit(solution)/shard_map/psum | solution.py:45
  195.9 17.3 %copy.41 = f32[2,256,256]{0,2,1:T(8,128)} copy(f32[2,256,256]{2,1,0:T(8,128)} %all-reduce.7.cloned.1.call-done) | data formatting | bytes 1048576 | tf_op jit(solution)/shard_map/psum | solution.py:45
  213.2 3.0 gather_fusion.1
  220.1 1.9 fusion.21
  230.7 3.1 fusion.97
  235.7 16.9 %collective-permute-done.1 = f32[1536,128]{0,1:T(8,128)S(1)} collective-permute-done((f32[1536,128]{0,1:T(8,128)S(1)}, f32[1536,128]{0,1:T(8,128)S(1)}, u32[]{:S(2)}, u32[]{:S(2)}) %collective-permute-start.1) | collective-permute-done | bytes 786464 | tf_op jit(solution)/shard_map/ppermute | solution.py:14
  252.8 3.9 fusion.98
  256.8 55.7 %all-reduce.9.cloned.1.call-done = f32[2,256,256]{2,1,0:T(8,128)} async-done(((f32[2,256,256]{2,1,0:T(8,128)}), f32[2,256,256]{2,1,0:T(8,128)}) %all-reduce.9.cloned.1.call-update) | async-done | bytes 524304 | tf_op jit(solution)/shard_map/psum | solution.py:45
  312.4 17.3 %copy.48 = f32[2,256,256]{0,2,1:T(8,128)} copy(f32[2,256,256]{2,1,0:T(8,128)} %all-reduce.9.cloned.1.call-done) | data formatting | bytes 1048576 | tf_op jit(solution)/shard_map/psum | solution.py:45
  329.7 3.0 gather_fusion.2
  336.7 1.9 fusion.16
  347.2 3.1 fusion.101
  352.2 16.9 %collective-permute-done.2 = f32[1536,128]{0,1:T(8,128)S(1)} collective-permute-done((f32[1536,128]{0,1:T(8,128)S(1)}, f32[1536,128]{0,1:T(8,128)S(1)}, u32[]{:S(2)}, u32[]{:S(2)}) %collective-permute-start.2) | collective-permute-done | bytes 786464 | tf_op jit(solution)/shard_map/ppermute | solution.py:14
  369.4 3.9 fusion.102
  373.3 55.7 %all-reduce.11.cloned.1.call-done = f32[2,256,256]{2,1,0:T(8,128)} async-done(((f32[2,256,256]{2,1,0:T(8,128)}), f32[2,256,256]{2,1,0:T(8,128)}) %all-reduce.11.cloned.1.call-update) | async-done | bytes 524304 | tf_op jit(solution)/shard_map/psum | solution.py:45
  429.0 17.3 %copy.55 = f32[2,256,256]{0,2,1:T(8,128)} copy(f32[2,256,256]{2,1,0:T(8,128)} %all-reduce.11.cloned.1.call-done) | data formatting | bytes 1048576 | tf_op jit(solution)/shard_map/psum | solution.py:45
  446.3 3.0 gather_fusion.3
  453.2 1.9 fusion.11
  463.8 4.7 fusion.4
  468.5 13.7 %psum.39 = f32[512]{0:T(512)S(1)} all-reduce(f32[512]{0:T(512)S(1)} %bitcast.301), channel_id=1, replica_groups=mesh['rows'=8,'pairs'=4] {'rows'}, use_global_device_ids=true, to_apply=%region_9.10 | all-reduce | flops 512 | bytes 4096 | tf_op jit(solution)/shard_map/psum | solution.py:53
  482.2 2.2 bitcast_multiply_fusion
  484.9 74.3 %all_to_all.5 = f32[32,1,16,1536]{3,2,1,0:T(8,128)S(1)} all-to-all(f32[32,1,16,1536]{3,2,1,0:T(8,128)S(1)} %fusion.45), channel_id=1, replica_groups=mesh['rows'=8,'pairs'=4] {'rows','pairs'}, dimensions={0} | all-to-all | bytes 6291456 | tf_op jit(solution)/shard_map/all_to_all | solution.py:63
  561.1 3.4 copy.74
  (121 shorter events, 60.0 us)
Async XLA Ops:
  6.5 70.5 %all-reduce.5.cloned.1.call-start = ((), (), s32[]{:S(2)}) async-start(), calls=%async_computation.1 | async-start | bytes 1048576 | tf_op jit(solution)/shard_map/psum | solution.py:45
  17.7 178.3 %all-reduce.7.cloned.1.call-start = ((), (), s32[]{:S(2)}) async-start(), calls=%async_computation.2 | async-start | bytes 1048576 | tf_op jit(solution)/shard_map/psum | solution.py:45
  100.1 3.3 copy-start
  100.1 3.9 copy-start.4
  117.6 18.5 %collective-permute-start = (f32[1536,128]{0,1:T(8,128)S(1)}, f32[1536,128]{0,1:T(8,128)S(1)}, u32[]{:S(2)}, u32[]{:S(2)}) collective-permute-start(f32[1536,128]{0,1:T(8,128)S(1)} %get-tuple-element.16), channel_id=1, source_target_pairs={{3,0},{0,1},{1,2},{2,3},{7,4},{4,5},{5,6},{6,7},{11,8},{8,9},{9,10... | collective-permute-start | bytes 2359304 | tf_op jit(solution)/shard_map/ppermute | solution.py:14
  140.1 172.3 %all-reduce.9.cloned.1.call-start = ((), (), s32[]{:S(2)}) async-start(), calls=%async_computation.3 | async-start | bytes 1048576 | tf_op jit(solution)/shard_map/psum | solution.py:45
  218.7 3.3 copy-start.1
  218.7 3.9 copy-start.5
  234.0 18.6 %collective-permute-start.1 = (f32[1536,128]{0,1:T(8,128)S(1)}, f32[1536,128]{0,1:T(8,128)S(1)}, u32[]{:S(2)}, u32[]{:S(2)}) collective-permute-start(f32[1536,128]{0,1:T(8,128)S(1)} %get-tuple-element.12), channel_id=1, source_target_pairs={{3,0},{0,1},{1,2},{2,3},{7,4},{4,5},{5,6},{6,7},{11,8},{8,9},{9,10... | collective-permute-start | bytes 2359304 | tf_op jit(solution)/shard_map/ppermute | solution.py:14
  256.7 172.3 %all-reduce.11.cloned.1.call-start = ((), (), s32[]{:S(2)}) async-start(), calls=%async_computation.4 | async-start | bytes 1048576 | tf_op jit(solution)/shard_map/psum | solution.py:45
  335.2 3.3 copy-start.2
  335.3 3.9 copy-start.6
  350.5 18.7 %collective-permute-start.2 = (f32[1536,128]{0,1:T(8,128)S(1)}, f32[1536,128]{0,1:T(8,128)S(1)}, u32[]{:S(2)}, u32[]{:S(2)}) collective-permute-start(f32[1536,128]{0,1:T(8,128)S(1)} %get-tuple-element.8), channel_id=1, source_target_pairs={{3,0},{0,1},{1,2},{2,3},{7,4},{4,5},{5,6},{6,7},{11,8},{8,9},{9,10... | collective-permute-start | bytes 2359304 | tf_op jit(solution)/shard_map/ppermute | solution.py:14
  451.8 3.3 copy-start.3
  451.8 3.9 copy-start.7
  463.8 18.4 %copy-start.8 = (f32[512]{0:T(512)S(1)}, f32[512]{0:T(512)}, u32[]{:S(2)}) copy-start(f32[512]{0:T(512)} %param.7) | copy-start | bytes 6148
Sparse Core Ops, SparseCore 0:
  17.8 59.2 all-reduce.4
  140.3 55.6 all-reduce.6
  256.8 55.5 all-reduce.8
  373.4 55.5 all-reduce.10
